TPU v7x, 32 devices: a whole 2x2x4 slice. The times are simulated.
32 devices in a mesh: expert: 8 (over y, x, core), dp: 4 (over z).
Axes of the slice: x: 2, y: 2, z: 4, core: 2. Of those that a mesh axis runs over, the one named last changes fastest.
Arguments:
- tokens: bfloat16 [4096, 1024], P(('expert', 'dp')), may hold values from -6 to 6
- expert_ids: int32 [4096, 8], P(('expert', 'dp')), may hold values from 0 to 15, all different within a row; in each aligned block of 128 rows (0 to 127, 128 to 255, ...) at most 96 rows name the same one
- combine_weights: float32 [4096, 8], P(('expert', 'dp')), may hold values from 0.2 to 1
- lift_weights: bfloat16 [16, 1024, 768], P('expert', 'dp'), may hold values from -0.1875 to 0.1875
- down_weights: bfloat16 [16, 384, 1024], P('expert', None, 'dp'), may hold values from -0.3125 to 0.3125
- cotangent: bfloat16 [4096, 1024], P(('expert', 'dp')), may hold values from -1.5 to 1.5
Outputs:
- layer_output: bfloat16 [4096, 1024], P(('expert', 'dp'))
- token_grads: bfloat16 [4096, 1024], P(('expert', 'dp'))
- lift_grads: bfloat16 [16, 1024, 768], P('expert', 'dp')
- down_grads: bfloat16 [16, 384, 1024], P('expert', None, 'dp')
Inputs may be any that keep to these rules, and one draw needn't show every extreme that they name: `expert_ids`: each row names 8 different experts. Among the 128 rows of one device, no expert is named more than 96 times, and in every draw some expert is named exactly 96 times in some device's rows.
All inputs are finite; a program needn't handle non-finite values.
Results may differ from a plain program's by a relative error of at most 0.02.
Values may be sent and summed in bfloat16 or wider, within the bound.
A program may use at most 64 MiB of HBM per device.

v0:
```python
import jax
import jax.numpy as jnp
from jax import lax
from jax.sharding import PartitionSpec as P


def swish_parts(gate_part):
    sigmoid_val = jax.nn.sigmoid(gate_part)
    return (gate_part * sigmoid_val, sigmoid_val * (1.0 + gate_part * (1.0 - sigmoid_val)))


def collect(returned, target, tok_rows, top_count):
    flat_back = returned.reshape(-1, returned.shape[-1])
    return flat_back[target].reshape(tok_rows, top_count, returned.shape[-1])


def shards(tokens, expert_ids, combine_weights, lift_weights, down_weights, cotangent):
    tok_rows, top_count = expert_ids.shape
    local_experts = lift_weights.shape[0]
    hidden_width = down_weights.shape[1]
    model_width = tokens.shape[1]
    owners = lax.axis_size("expert")
    all_experts = local_experts * owners
    capacity = max(2, 3 * tok_rows * top_count // (2 * all_experts))
    slot_total = tok_rows * top_count
    flat_ids = expert_ids.reshape(-1)
    onehot = (flat_ids[:, None] == jnp.arange(all_experts, dtype=jnp.int32)[None, :]).astype(
        jnp.int32
    )
    ranking = jnp.sum(jnp.cumsum(onehot, axis=0) * onehot, axis=1) - 1
    target = (flat_ids % local_experts * owners + flat_ids // local_experts) * capacity + ranking
    source_of = (
        jnp.full((all_experts * capacity,), -1, jnp.int32)
        .at[target]
        .set(jnp.arange(slot_total, dtype=jnp.int32))
    )
    filled = (source_of >= 0)[:, None]
    source_slot = jnp.maximum(source_of, 0)
    source_row = source_slot // top_count
    slot_gates = combine_weights.reshape(-1)[source_slot]
    buffer_shape = (local_experts, owners, capacity, model_width)
    rows_shape = (local_experts, owners * capacity, model_width)
    send_rows = jnp.where(filled, tokens[source_row], jnp.zeros((), jnp.bfloat16)).reshape(
        buffer_shape
    )
    send_back = jnp.where(
        filled, slot_gates[:, None] * cotangent[source_row].astype(jnp.float32), 0.0
    )
    send_back = send_back.astype(jnp.bfloat16).reshape(buffer_shape)
    recv_rows = lax.all_to_all(
        send_rows, "expert", split_axis=1, concat_axis=1, tiled=True
    ).reshape(rows_shape)
    part_rows = recv_rows
    portion = lax.all_gather(lift_weights, "dp", axis=1, tiled=True)
    gate_term = jnp.einsum(
        "erd,edf->erf", part_rows, portion[:, :, :hidden_width], preferred_element_type=jnp.float32
    )
    up_term = jnp.einsum(
        "erd,edf->erf", part_rows, portion[:, :, hidden_width:], preferred_element_type=jnp.float32
    )
    gate_term, up_term = (gate_term, up_term)
    swished, slopes = swish_parts(gate_term)
    activated = (swished * up_term).astype(jnp.bfloat16)
    portion = lax.all_gather(down_weights, "dp", axis=2, tiled=True)
    result = jnp.stack(
        [
            jnp.dot(activated[expert], portion[expert], preferred_element_type=jnp.float32).astype(
                jnp.bfloat16
            )
            for expert in range(local_experts)
        ]
    )
    returned = lax.all_to_all(
        result.reshape(buffer_shape), "expert", split_axis=1, concat_axis=1, tiled=True
    )
    recv_back = lax.all_to_all(
        send_back, "expert", split_axis=1, concat_axis=1, tiled=True
    ).reshape(rows_shape)
    part_back = recv_back
    act_grad = jnp.einsum(
        "ern,efn->erf",
        part_back,
        lax.all_gather(down_weights, "dp", axis=2, tiled=True),
        preferred_element_type=jnp.float32,
    )
    grad_gate = (act_grad * up_term * slopes).astype(jnp.bfloat16)
    grad_up = (act_grad * swished).astype(jnp.bfloat16)
    portion = lax.all_gather(lift_weights, "dp", axis=1, tiled=True)
    contract = (((1,), (1,)), ((), ()))
    outputs = []
    for expert in range(local_experts):
        first = lax.dot_general(
            grad_gate[expert],
            portion[expert, :, :hidden_width],
            contract,
            preferred_element_type=jnp.float32,
        )
        second = lax.dot_general(
            grad_up[expert],
            portion[expert, :, hidden_width:],
            contract,
            preferred_element_type=jnp.float32,
        )
        outputs.append((first + second).astype(jnp.bfloat16))
    input_grads = jnp.stack(outputs)
    returned_grads = lax.all_to_all(
        input_grads.reshape(buffer_shape), "expert", split_axis=1, concat_axis=1, tiled=True
    )
    picked = collect(returned, target, tok_rows, top_count)
    layer_output = jnp.sum(combine_weights[:, :, None] * picked.astype(jnp.float32), axis=1).astype(
        jnp.bfloat16
    )
    grads_picked = collect(returned_grads, target, tok_rows, top_count)
    token_grads = jnp.sum(grads_picked.astype(jnp.float32), axis=1).astype(jnp.bfloat16)
    part_rows = recv_rows
    part_back = recv_back
    gate_grad = jnp.einsum("ern,erf->nef", part_rows, grad_gate, preferred_element_type=jnp.float32)
    up_grad = jnp.einsum("ern,erf->nef", part_rows, grad_up, preferred_element_type=jnp.float32)
    down_grad = jnp.einsum("ern,erf->nef", part_back, activated, preferred_element_type=jnp.float32)
    summed = lax.psum_scatter(
        jnp.concatenate([gate_grad, up_grad, down_grad], axis=2).astype(jnp.bfloat16),
        "dp",
        scatter_dimension=0,
        tiled=True,
    ).astype(jnp.float32)
    lift_grads = jnp.transpose(summed[:, :, : 2 * hidden_width], (1, 0, 2)).astype(jnp.bfloat16)
    down_grads = jnp.transpose(summed[:, :, 2 * hidden_width :], (1, 2, 0)).astype(jnp.bfloat16)
    return (layer_output, token_grads, lift_grads, down_grads)


def solution(mesh):
    in_specs = (
        P(("expert", "dp"), None),
        P(("expert", "dp"), None),
        P(("expert", "dp"), None),
        P("expert", "dp", None),
        P("expert", None, "dp"),
        P(("expert", "dp"), None),
    )
    out_specs = (
        P(("expert", "dp"), None),
        P(("expert", "dp"), None),
        P("expert", "dp", None),
        P("expert", None, "dp"),
    )
    return jax.shard_map(shards, mesh=mesh, in_specs=in_specs, out_specs=out_specs, check_vma=False)
```

profile of v0, /device:TPU:0, one launch (start us, length us, event | category | flops | bytes accessed | tf_op | source)
XLA Modules:
  0.0 261.8 jit_solution(11548749178795557380)
XLA Ops:
  9.9 4.5 %reduce-window.6 = s32[16,8,128]{2,1,0:T(8,128)S(1)} reduce-window(s32[16,8,128]{2,1,0:T(8,128)S(1)} %fusion.15, s32[]{:T(128)} %constant.56.clone.1), window={size=1x1x128 pad=0_0x0_0x127_0}, to_apply=%region_0.0 | reduce-window | flops 2080768 | bytes 131076 | tf_op jit(solution)/shard_map/reduce-window
  14.9 4.3 %scatter_custom_fusion = s32[1536]{0:T(1024)S(1)} fusion(s32[1024]{0:T(1024)S(1)} %bitcast.113, s32[1024]{0:T(1024)S(1)} %iota.11, s32[]{:T(128)} %constant.55.clone.1), kind=kCustom, calls=%fused_computation.75 | custom fusion | bytes 6148 | tf_op jit(solution)/shard_map/scatter | solution.py:35
  19.4 5.9 %gather_fusion.2 = f32[1536]{0:T(1024)S(1)} fusion(f32[1024]{0:T(1024)S(1)} %reshape.211, s32[2048]{0:T(1024)S(1)} %get-tuple-element.25), kind=kCustom, calls=%fused_computation.2 | custom fusion | bytes 18432 | tf_op jit(solution)/shard_map/gather | solution.py:40
  25.3 5.1 %gather_fusion.3 = bf16[1536,1024]{1,0:T(8,128)(2,1)S(1)} fusion(bf16[128,1024]{1,0:T(8,128)(2,1)S(1)} %copy-done, s32[2048]{0:T(1024)S(1)} %get-tuple-element.26), kind=kCustom, calls=%fused_computation.3 | custom fusion | bytes 6297600 | tf_op jit(solution)/shard_map/gather | solution.py:47
  30.4 2.2 fusion.1
  32.6 5.3 %all-to-all-start.2 = ((bf16[2,8,96,1024]{3,2,0,1:T(8,128)(2,1)}), bf16[2,8,96,1024]{3,2,0,1:T(8,128)(2,1)S(1)}, u32[]{:S(2)}, u32[]{:S(2)}) async-start(bf16[2,8,96,1024]{3,2,0,1:T(8,128)(2,1)} %fusion.1), calls=%async_computation.2 | async-start | bytes 6291456 | tf_op jit(solution)/shard_map/all_to_all | solution.py:76
  38.0 5.9 %gather_fusion = bf16[1536,1024]{1,0:T(8,128)(2,1)} fusion(bf16[128,1024]{1,0:T(8,128)(2,1)S(1)} %copy-done.2, s32[2048]{0:T(1024)S(1)} %get-tuple-element.26), kind=kCustom, calls=%fused_computation | custom fusion | bytes 6297600 | tf_op jit(solution)/shard_map/gather | solution.py:43
  43.8 3.3 %copy_select_fusion = bf16[2,8,96,1024]{3,2,0,1:T(8,128)(2,1)} fusion(bf16[2,8,96,1024]{3,2,1,0:T(8,128)(2,1)} %bitcast.99, pred[2,8,96]{2,0,1:T(4,128)(4,1)S(1)} %copy.55), kind=kLoop, calls=%fused_computation.14 | loop fusion | flops 1572864 | bytes 6292992 | tf_op jit(solution)/shard_map/jit(_where)/select_n | solution.py:43
  47.1 28.7 %all-to-all-done.2 = bf16[2,8,96,1024]{3,2,0,1:T(8,128)(2,1)S(1)} async-done(((bf16[2,8,96,1024]{3,2,0,1:T(8,128)(2,1)}), bf16[2,8,96,1024]{3,2,0,1:T(8,128)(2,1)S(1)}, u32[]{:S(2)}, u32[]{:S(2)}) %all-to-all-start.2) | async-done | bytes 3145760 | tf_op jit(solution)/shard_map/all_to_all | solution.py:76
  75.8 4.4 %all-to-all-start = ((bf16[2,8,96,1024]{3,2,0,1:T(8,128)(2,1)}), bf16[2,8,96,1024]{3,2,0,1:T(8,128)(2,1)}, u32[]{:S(2)}, u32[]{:S(2)}) async-start(bf16[2,8,96,1024]{3,2,0,1:T(8,128)(2,1)} %copy_select_fusion), calls=%async_computation | async-start | bytes 6291456 | tf_op jit(solution)/shard_map/all_to_all | solution.py:50
  81.2 2.2 copy.64
  83.5 34.6 %all-to-all-done = bf16[2,8,96,1024]{3,2,0,1:T(8,128)(2,1)} async-done(((bf16[2,8,96,1024]{3,2,0,1:T(8,128)(2,1)}), bf16[2,8,96,1024]{3,2,0,1:T(8,128)(2,1)}, u32[]{:S(2)}, u32[]{:S(2)}) %all-to-all-start) | async-done | bytes 3145760 | tf_op jit(solution)/shard_map/all_to_all | solution.py:50
  118.1 2.4 copy.57
  122.1 4.7 %fusion.4 = f32[2,768,384]{2,1,0:T(8,128)} fusion(bf16[2,768,1024]{2,1,0:T(8,128)(2,1)S(1)} %bitcast.105, bf16[2,1024,768]{2,1,0:T(8,128)(2,1)} %all-gather.3.cloned.1.call-done), kind=kOutput, calls=%fused_computation.28 | convolution fusion | flops 1207959552 | bytes 7077888 | tf_op jit(solution)/shard_map/erd,edf->erf/dot_general | solution.py:58
  126.9 5.3 %fusion.6 = f32[2,768,384]{2,1,0:T(8,128)} fusion(bf16[2,768,1024]{2,1,0:T(8,128)(2,1)} %bitcast.106, bf16[2,1024,768]{2,1,0:T(8,128)(2,1)S(1)} %copy-done.8), kind=kOutput, calls=%fused_computation.30 | convolution fusion | flops 1207959552 | bytes 7077888 | tf_op jit(solution)/shard_map/erd,edf->erf/dot_general | solution.py:55
  132.2 5.3 %multiply_convert_fusion = (bf16[2,768,384]{2,1,0:T(8,128)(2,1)S(1)}, bf16[2,768,384]{2,1,0:T(8,128)(2,1)S(1)}, bf16[2,768,384]{2,1,0:T(8,128)(2,1)S(1)}) fusion(f32[2,768,384]{2,1,0:T(8,128)} %fusion.6, f32[2,768,384]{2,1,0:T(8,128)} %fusion.4, bf16[2,768,1024]{2,1,0:T(8,128)(2,1)S(1)} %bitcast.103, bf16[2,384,1024]{2,1,0:T(8,128)(2,1)} %all-gather.5.cloned.1.call-done), kind=kOutput, calls=%fused_computation.17 | convolution fusion | flops 1216806912 | bytes 12976128 | tf_op jit(solution)/shard_map/ern,efn->erf/dot_general | solution.py:80
  143.7 2.4 pad_maximum_fusion
  149.8 2.0 pad_maximum_fusion.1
  151.8 3.9 %all-to-all-start.1 = ((bf16[2,8,96,1024]{3,2,0,1:T(8,128)(2,1)}), bf16[2,8,96,1024]{3,2,0,1:T(8,128)(2,1)S(1)}, u32[]{:S(2)}, u32[]{:S(2)}) async-start(bf16[2,8,96,1024]{3,2,0,1:T(8,128)(2,1)} %pad_maximum_fusion.1), calls=%async_computation.1 | async-start | bytes 6291456 | tf_op jit(solution)/shard_map/all_to_all | solution.py:73
  155.7 2.5 fusion.11
  161.7 1.9 pad_maximum_fusion.2
  163.6 29.7 %all-to-all-done.1 = bf16[2,8,96,1024]{3,2,0,1:T(8,128)(2,1)S(1)} async-done(((bf16[2,8,96,1024]{3,2,0,1:T(8,128)(2,1)}), bf16[2,8,96,1024]{3,2,0,1:T(8,128)(2,1)S(1)}, u32[]{:S(2)}, u32[]{:S(2)}) %all-to-all-start.1) | async-done | bytes 3145760 | tf_op jit(solution)/shard_map/all_to_all | solution.py:73
  193.3 1.8 copy-done.3
  195.0 4.5 %all-to-all-start.3 = ((bf16[2,8,96,1024]{3,2,0,1:T(8,128)(2,1)}), bf16[2,8,96,1024]{3,2,0,1:T(8,128)(2,1)}, u32[]{:S(2)}, u32[]{:S(2)}) async-start(bf16[2,8,96,1024]{3,2,0,1:T(8,128)(2,1)} %pad_maximum_fusion.2), calls=%async_computation.3 | async-start | bytes 6291456 | tf_op jit(solution)/shard_map/all_to_all | solution.py:106
  199.5 2.4 copy.60
  201.9 5.3 %gather_fusion.1 = bf16[1024,1024]{1,0:T(8,128)(2,1)} fusion(bf16[1536,1024]{1,0:T(8,128)(2,1)S(1)} %bitcast.98, s32[1024]{0:T(1024)S(1)} %broadcast_clamp_fusion), kind=kCustom, calls=%fused_computation.1 | custom fusion | bytes 4198400 | tf_op jit(solution)/shard_map/gather | solution.py:14
  207.3 30.1 %all-to-all-done.3 = bf16[2,8,96,1024]{3,2,0,1:T(8,128)(2,1)} async-done(((bf16[2,8,96,1024]{3,2,0,1:T(8,128)(2,1)}), bf16[2,8,96,1024]{3,2,0,1:T(8,128)(2,1)}, u32[]{:S(2)}, u32[]{:S(2)}) %all-to-all-start.3) | async-done | bytes 3145760 | tf_op jit(solution)/shard_map/all_to_all | solution.py:106
  237.4 2.4 copy.67
  239.8 5.4 %gather_fusion.4 = bf16[1024,1024]{1,0:T(8,128)(2,1)} fusion(bf16[1536,1024]{1,0:T(8,128)(2,1)S(1)} %bitcast.97, s32[1024]{0:T(1024)S(1)} %broadcast_clamp_fusion), kind=kCustom, calls=%fused_computation.4 | custom fusion | bytes 4198400 | tf_op jit(solution)/shard_map/gather | solution.py:14
  245.2 3.9 %bitcast_reduce_fusion = bf16[128,1024]{1,0:T(8,128)(2,1)} fusion(bf16[1024,1024]{1,0:T(8,128)(2,1)} %gather_fusion.4), kind=kLoop, calls=%fused_computation.22 | loop fusion | flops 917504 | bytes 2359296 | tf_op jit(solution)/shard_map/reduce_sum | solution.py:114
  249.1 2.1 fusion.2
  253.5 1.8 slice_bitcast_fusion.25
  (77 shorter events, 21.5 us)
Async XLA Ops:
  7.2 18.2 %copy-start = (bf16[128,1024]{1,0:T(8,128)(2,1)S(1)}, bf16[128,1024]{1,0:T(8,128)(2,1)}, u32[]{:S(2)}) copy-start(bf16[128,1024]{1,0:T(8,128)(2,1)} %param.11) | copy-start | bytes 786436
  7.2 113.3 %all-gather.3.cloned.1.call-start = ((), (), s32[]{:S(2)}) async-start(), calls=%async_computation.5 | async-start | bytes 3932160 | tf_op jit(solution)/shard_map/all_gather | solution.py:54
  32.6 5.3 %copy-start.2 = (bf16[128,1024]{1,0:T(8,128)(2,1)S(1)}, bf16[128,1024]{1,0:T(8,128)(2,1)}, u32[]{:S(2)}) copy-start(bf16[128,1024]{1,0:T(8,128)(2,1)} %param.6) | copy-start | bytes 786436
  32.6 43.2 %all-to-all-start.2 = ((bf16[2,8,96,1024]{3,2,0,1:T(8,128)(2,1)}), bf16[2,8,96,1024]{3,2,0,1:T(8,128)(2,1)S(1)}, u32[]{:S(2)}, u32[]{:S(2)}) async-start(bf16[2,8,96,1024]{3,2,0,1:T(8,128)(2,1)} %fusion.1), calls=%async_computation.2 | async-start | bytes 6291456 | tf_op jit(solution)/shard_map/all_to_all | solution.py:76
  75.8 42.3 %all-to-all-start = ((bf16[2,8,96,1024]{3,2,0,1:T(8,128)(2,1)}), bf16[2,8,96,1024]{3,2,0,1:T(8,128)(2,1)}, u32[]{:S(2)}, u32[]{:S(2)}) async-start(bf16[2,8,96,1024]{3,2,0,1:T(8,128)(2,1)} %copy_select_fusion), calls=%async_computation | async-start | bytes 6291456 | tf_op jit(solution)/shard_map/all_to_all | solution.py:50
  80.2 52.0 %all-gather.5.cloned.1.call-start = ((), (), s32[]{:S(2)}) async-start(), calls=%async_computation.6 | async-start | bytes 1966080 | tf_op jit(solution)/shard_map/all_gather | solution.py:64
  81.0 170.1 %reduce-scatter.2.cloned.1.call-start = ((), (), s32[]{:S(2)}) async-start(), calls=%async_computation.7 | async-start | bytes 5898240 | tf_op jit(solution)/shard_map/reduce_scatter | solution.py:120
  120.5 1.7 copy-start.6
  122.1 4.7 %copy-start.8 = (bf16[2,1024,768]{2,1,0:T(8,128)(2,1)S(1)}, bf16[2,1024,768]{2,1,0:T(8,128)(2,1)}, u32[]{:S(2)}) copy-start(bf16[2,1024,768]{2,1,0:T(8,128)(2,1)} %all-gather.3.cloned.1.call-done) | copy-start | bytes 9437188
  126.9 5.3 %copy-start.5 = (bf16[2,8,96,1024]{3,2,1,0:T(8,128)(2,1)S(1)}, bf16[2,8,96,1024]{3,2,1,0:T(8,128)(2,1)}, u32[]{:S(2)}) copy-start(bf16[2,8,96,1024]{3,2,1,0:T(8,128)(2,1)} %copy.64) | copy-start | bytes 9437188
  137.6 1.5 copy-start.15
  137.6 1.5 copy-start.10
  137.6 4.7 %copy-start.12 = (bf16[2,768,384]{2,1,0:T(8,128)(2,1)}, bf16[2,768,384]{2,1,0:T(8,128)(2,1)S(1)}, u32[]{:S(2)}) copy-start(bf16[2,768,384]{2,1,0:T(8,128)(2,1)S(1)} %get-tuple-element.21) | copy-start | bytes 3538948
  137.6 3.2 %copy-start.7 = (bf16[2,8,96,1024]{3,2,1,0:T(8,128)(2,1)S(1)}, bf16[2,8,96,1024]{3,2,1,0:T(8,128)(2,1)}, u32[]{:S(2)}) copy-start(bf16[2,8,96,1024]{3,2,1,0:T(8,128)(2,1)} %copy-done.6) | copy-start | bytes 9437188
  146.1 1.4 copy-start.14
  146.1 1.7 copy-start.16
  151.8 41.4 %all-to-all-start.1 = ((bf16[2,8,96,1024]{3,2,0,1:T(8,128)(2,1)}), bf16[2,8,96,1024]{3,2,0,1:T(8,128)(2,1)S(1)}, u32[]{:S(2)}, u32[]{:S(2)}) async-start(bf16[2,8,96,1024]{3,2,0,1:T(8,128)(2,1)} %pad_maximum_fusion.1), calls=%async_computation.1 | async-start | bytes 6291456 | tf_op jit(solution)/shard_map/all_to_all | solution.py:73
  155.7 2.5 copy-start.9
  155.7 2.6 %copy-start.13 = (bf16[2,768,384]{2,1,0:T(8,128)(2,1)S(1)}, bf16[2,768,384]{2,1,0:T(8,128)(2,1)}, u32[]{:S(2)}) copy-start(bf16[2,768,384]{2,1,0:T(8,128)(2,1)} %copy-done.12) | copy-start | bytes 3538948
  158.3 1.3 copy-start.11
  193.3 1.8 copy-start.3
  195.0 42.4 %all-to-all-start.3 = ((bf16[2,8,96,1024]{3,2,0,1:T(8,128)(2,1)}), bf16[2,8,96,1024]{3,2,0,1:T(8,128)(2,1)}, u32[]{:S(2)}, u32[]{:S(2)}) async-start(bf16[2,8,96,1024]{3,2,0,1:T(8,128)(2,1)} %pad_maximum_fusion.2), calls=%async_computation.3 | async-start | bytes 6291456 | tf_op jit(solution)/shard_map/all_to_all | solution.py:106
  245.2 3.9 %copy-start.4 = (bf16[1024,1024]{1,0:T(8,128)(2,1)S(1)}, bf16[1024,1024]{1,0:T(8,128)(2,1)}, u32[]{:S(2)}) copy-start(bf16[1024,1024]{1,0:T(8,128)(2,1)} %gather_fusion.1) | copy-start | bytes 6291460
  245.2 10.1 %copy-start.1 = (bf16[128,1024]{1,0:T(8,128)(2,1)S(1)}, bf16[128,1024]{1,0:T(8,128)(2,1)}, u32[]{:S(2)}) copy-start(bf16[128,1024]{1,0:T(8,128)(2,1)} %param.11) | copy-start | bytes 786436
Sparse Core Ops, SparseCore 0:
  9.6 66.1 all-gather.2
  82.6 39.2 all-gather.4
  146.2 84.6 reduce-scatter.1
where the time goes:
time: 263 us; the launch traced here: 262 us
  waiting for transfers between devices  125 us (48%)
  local copies, waits for them, and re-layouts  54.9 us (21%)
  matrix products  27.3 us (10%)
  other arithmetic  22.5 us (9%)
  starting transfers between devices  18.4 us (7%)
  between operations  14.1 us (5%)
    all_to_all x1, waiting for transfers between devices, shards(): lax.all_to_all(send_rows, 'expert', split_axis=1, concat_axis=1, tiled=True)  34.6 us
    all_to_all x1, waiting for transfers between devices, shards(): lax.all_to_all(input_grads.reshape(buffer_shape), 'expert', split_axis=1,...  30.1 us
    all_to_all x1, waiting for transfers between devices, shards(): lax.all_to_all(result.reshape(buffer_shape), 'expert', split_axis=1, conc...  29.7 us
    all_to_all x1, waiting for transfers between devices, shards(): lax.all_to_all(send_back, 'expert', split_axis=1, concat_axis=1, tiled=True)  28.7 us
    gather x2, local copies, waits for them, and re-layouts, collect(): return flat_back[target].reshape(tok_rows, top_count, returned.shape[-1])  10.7 us
    unnamed x37, local copies, waits for them, and re-layouts  9.93 us
    gather x1, local copies, waits for them, and re-layouts, shards(): tokens[source_row]  5.86 us
    gather x1, local copies, waits for them, and re-layouts, shards(): slot_gates = combine_weights.reshape(-1)[source_slot]  5.85 us
  transfers between devices with their start and end apart: 7, of which 4 were waited for; matrix products, arithmetic and copies ran while one was open for 31% of the time, Pallas kernels for 0%

commit v1 on v0

--- a/solution.py
+++ b/solution.py
@@ -14,7 +14,7 @@
     return flat_back[target].reshape(tok_rows, top_count, returned.shape[-1])
 
 
-def shards(tokens, expert_ids, combine_weights, lift_weights, down_weights, cotangent):
+def slot_shards(tokens, expert_ids, combine_weights, lift_weights, down_weights, cotangent):
     tok_rows, top_count = expert_ids.shape
     local_experts = lift_weights.shape[0]
     hidden_width = down_weights.shape[1]
@@ -128,6 +128,84 @@
     return (layer_output, token_grads, lift_grads, down_grads)
 
 
+def dot(left, right, left_dim, right_dim):
+    return lax.dot_general(
+        left, right, (((left_dim,), (right_dim,)), ((), ())), preferred_element_type=jnp.float32
+    )
+
+
+def spread(block, owners):
+    copies = jnp.broadcast_to(block[None], (owners,) + block.shape)
+    return lax.all_to_all(copies, "expert", split_axis=0, concat_axis=0, tiled=True)
+
+
+def dense_shards(tokens, expert_ids, combine_weights, lift_weights, down_weights, cotangent):
+    tok_rows, top_count = expert_ids.shape
+    local_experts = lift_weights.shape[0]
+    hidden_width = down_weights.shape[1]
+    model_width = tokens.shape[1]
+    owners = lax.axis_size("expert")
+    all_rows = owners * tok_rows
+    all_experts = owners * local_experts
+    both = jnp.concatenate([lift_weights, jnp.transpose(down_weights, (0, 2, 1))], axis=2)
+    both = lax.all_gather(both, "dp", axis=1, tiled=True)
+    lift, down = both[:, :, : 2 * hidden_width], both[:, :, 2 * hidden_width :]
+    named = expert_ids[:, :, None] == jnp.arange(all_experts, dtype=jnp.int32)[None, None, :]
+    dense = jnp.sum(jnp.where(named, combine_weights[:, :, None], 0.0), axis=1)
+    sent = jnp.transpose(dense.reshape(tok_rows, owners, local_experts), (1, 2, 0))
+    gates = lax.all_to_all(sent, "expert", split_axis=0, concat_axis=0, tiled=True)
+    gates = jnp.transpose(gates, (1, 0, 2)).reshape(local_experts, all_rows, 1)
+    rows = spread(tokens, owners).reshape(all_rows, model_width)
+    back = spread(cotangent, owners).reshape(all_rows, model_width).astype(jnp.float32)
+    weighted, grads, parts = [], [], []
+    for expert in range(local_experts):
+        gate_term = dot(rows, lift[expert, :, :hidden_width], 1, 0)
+        up_term = dot(rows, lift[expert, :, hidden_width:], 1, 0)
+        back_in = (gates[expert] * back).astype(jnp.bfloat16)
+        act_grad = dot(back_in, down[expert], 1, 0)
+        swished, slopes = swish_parts(gate_term)
+        activated = (swished * up_term).astype(jnp.bfloat16)
+        grad_gate = (act_grad * up_term * slopes).astype(jnp.bfloat16)
+        grad_up = (act_grad * swished).astype(jnp.bfloat16)
+        parts.append(
+            jnp.concatenate(
+                [dot(rows, grad_gate, 0, 0), dot(rows, grad_up, 0, 0), dot(back_in, activated, 0, 0)],
+                axis=1,
+            ).astype(jnp.bfloat16)
+        )
+        weighted.append((gates[expert] * activated.astype(jnp.float32)).astype(jnp.bfloat16))
+        grads.append((grad_gate, grad_up))
+    summed = lax.psum_scatter(jnp.stack(parts), "dp", scatter_dimension=1, tiled=True)
+    lift_grads = summed[:, :, : 2 * hidden_width]
+    down_grads = jnp.transpose(summed[:, :, 2 * hidden_width :], (0, 2, 1))
+
+    def returned(total):
+        blocks = total.astype(jnp.bfloat16).reshape(owners, tok_rows, model_width)
+        pieces = lax.all_to_all(blocks, "expert", split_axis=0, concat_axis=0, tiled=True)
+        return jnp.sum(pieces.astype(jnp.float32), axis=0).astype(jnp.bfloat16)
+
+    layer_output = returned(
+        sum(dot(weighted[expert], down[expert], 1, 1) for expert in range(local_experts))
+    )
+    token_grads = returned(
+        sum(
+            dot(grads[expert][0], lift[expert, :, :hidden_width], 1, 1)
+            + dot(grads[expert][1], lift[expert, :, hidden_width:], 1, 1)
+            for expert in range(local_experts)
+        )
+    )
+    return (layer_output, token_grads, lift_grads, down_grads)
+
+
+def shards(tokens, expert_ids, combine_weights, lift_weights, down_weights, cotangent):
+    tok_rows, top_count = expert_ids.shape
+    local_experts = lift_weights.shape[0]
+    all_experts = local_experts * lax.axis_size("expert")
+    capacity = max(2, 3 * tok_rows * top_count // (2 * all_experts))
+    plan = dense_shards if tok_rows <= local_experts * capacity else slot_shards
+    return plan(tokens, expert_ids, combine_weights, lift_weights, down_weights, cotangent)
+
+
 def solution(mesh):
     in_specs = (
         P(("expert", "dp"), None),

time: 263 us -> 234 us (0.89)
  local copies, waits for them, and re-layouts: 54.9 us -> 7.01 us
  blocking collectives: 0 us -> 38.9 us
  waiting for transfers between devices: 125 us -> 99.1 us
  matrix products: 27.3 us -> 42.2 us
  starting transfers between devices: 18.4 us -> 12.4 us
  other arithmetic: 22.5 us -> 18.7 us
    all_to_all x4 -> x3, waiting for transfers between devices: 123 us -> 66.9 us  [the longest x2 45.8 us: returned(): lax.all_to_all(blocks, 'expert', split_axis=0, concat_axis=0, tiled=True)]
    all_to_all x0 -> x2, blocking collectives: none -> 38.9 us  [the longest x1 29.1 us: spread(): lax.all_to_all(copies, 'expert', split_axis=0, concat_axis=0, tiled=True)]
    gather x5 -> x0, local copies, waits for them, and re-layouts: 27.5 us -> none  [the longest x2 10.7 us: collect(): return flat_back[target].reshape(tok_rows, top_count, returned.shape[-1])]
    all_gather x2 -> x1, waiting for transfers between devices: 0.02 us -> 20.6 us  [dense_shards(): both = lax.all_gather(both, 'dp', axis=1, tiled=True)]
    dot_general x12 -> x18, matrix products: 27.3 us -> 42.2 us  [dot(): lax.dot_general(left, right, (((left_dim,), (right_dim,)), ((), ())), pre...]
    reduce_scatter x1, waiting for transfers between devices: 0.01 us -> 11.6 us  [dense_shards(): lax.psum_scatter(jnp.stack(parts), 'dp', scatter_dimension=1, tiled=True)]
    all_to_all x4 -> x0, local copies, waits for them, and re-layouts: 9.34 us -> none  [the longest x1 2.37 us: shards(): lax.all_to_all(result.reshape(buffer_shape), 'expert', split_axis=1, conc...]
    unnamed x37, local copies, waits for them, and re-layouts: 9.93 us -> 2.04 us
  transfers between devices with their start and end apart: 7 -> 5, of which waited for: 4 -> 5; matrix products, arithmetic and copies ran while one was open for 31% -> 11% of each run, Pallas kernels for 0% -> 0%
where the time goes in v1:
time: 234 us; the launch traced here: 233 us
  waiting for transfers between devices  99.1 us (42%)
  matrix products  42.2 us (18%)
  blocking collectives  38.9 us (17%)
  other arithmetic  18.7 us (8%)
  between operations  14.4 us (6%)
  starting transfers between devices  12.4 us (5%)
  local copies, waits for them, and re-layouts  7.01 us (3%)
    all_to_all x2, waiting for transfers between devices, returned(): lax.all_to_all(blocks, 'expert', split_axis=0, concat_axis=0, tiled=True)  45.8 us
    dot_general x18, matrix products, dot(): lax.dot_general(left, right, (((left_dim,), (right_dim,)), ((), ())), pre...  42.2 us
    all_to_all x1, blocking collectives, spread(): lax.all_to_all(copies, 'expert', split_axis=0, concat_axis=0, tiled=True)  29.1 us
    all_to_all x1, waiting for transfers between devices, spread(): lax.all_to_all(copies, 'expert', split_axis=0, concat_axis=0, tiled=True)  21.1 us
    all_gather x1, waiting for transfers between devices, dense_shards(): both = lax.all_gather(both, 'dp', axis=1, tiled=True)  20.6 us
    reduce_scatter x1, waiting for transfers between devices, dense_shards(): lax.psum_scatter(jnp.stack(parts), 'dp', scatter_dimension=1, tiled=True)  11.6 us
    all_to_all x1, blocking collectives, dense_shards(): lax.all_to_all(sent, 'expert', split_axis=0, concat_axis=0, tiled=True)  9.71 us
    all_to_all x2, starting transfers between devices, returned(): lax.all_to_all(blocks, 'expert', split_axis=0, concat_axis=0, tiled=True)  8 us
  transfers between devices with their start and end apart: 5, of which 5 were waited for; matrix products, arithmetic and copies ran while one was open for 11% of the time, Pallas kernels for 0%

profile of v1, /device:TPU:0, one launch (start us, length us, event | category | flops | bytes accessed | tf_op | source)
XLA Modules:
  0.0 232.7 jit_solution(7642882282781053706)
XLA Ops:
  8.5 2.3 pad_maximum_fusion
  10.8 9.7 %all_to_all.25 = f32[8,2,128]{2,1,0:T(2,128)S(1)} all-to-all(f32[8,2,128]{2,1,0:T(2,128)S(1)} %bitcast.172), channel_id=1, replica_groups=mesh['expert'=8,'dp'=4] {'expert'}, dimensions={0} | all-to-all | bytes 16384 | tf_op jit(solution)/shard_map/all_to_all | solution.py:156
  20.8 29.1 %all_to_all.26 = bf16[8,128,1024]{2,1,0:T(8,128)(2,1)S(1)} all-to-all(bf16[8,128,1024]{2,1,0:T(8,128)(2,1)S(1)} %broadcast_in_dim.30), channel_id=1, replica_groups=mesh['expert'=8,'dp'=4] {'expert'}, dimensions={0} | all-to-all | bytes 4194304 | tf_op jit(solution)/shard_map/all_to_all | solution.py:139
  50.0 1.6 broadcast_in_dim.18
  51.5 4.3 %all-to-all-start.1 = ((bf16[8,128,1024]{2,1,0:T(8,128)(2,1)}), bf16[8,128,1024]{2,1,0:T(8,128)(2,1)}, u32[]{:S(2)}, u32[]{:S(2)}) async-start(bf16[8,128,1024]{2,1,0:T(8,128)(2,1)} %broadcast_in_dim.18), calls=%async_computation.1 | async-start | bytes 4194304 | tf_op jit(solution)/shard_map/all_to_all | solution.py:139
  56.0 2.7 %fusion = (bf16[8,128,1024]{2,1,0:T(8,128)(2,1)}, bf16[8,128,1024]{2,1,0:T(8,128)(2,1)}) fusion(bf16[8,128,1024]{2,1,0:T(8,128)(2,1)S(1)} %all_to_all.26, f32[8,128]{1,0:T(8,128)S(1)} %bitcast.165, f32[8,128]{1,0:T(8,128)S(1)} %bitcast.168), kind=kLoop, calls=%fused_computation.5 | loop fusion | flops 5242880 | bytes 6299648 | tf_op jit(solution)/shard_map/convert_element_type | solution.py:164
  58.7 2.7 %fusion.2 = (bf16[1024,1024]{1,0:T(8,128)(2,1)}, bf16[1024,1024]{1,0:T(8,128)(2,1)}) fusion(bf16[8,128,1024]{2,1,0:T(8,128)(2,1)S(1)} %all_to_all.26, f32[1024]{0:T(1024)S(1)} %bitcast.166, f32[1024]{0:T(1024)S(1)} %bitcast.169), kind=kLoop, calls=%fused_computation.7 | loop fusion | flops 5242880 | bytes 6299648 | tf_op jit(solution)/shard_map/convert_element_type | solution.py:164
  61.4 21.1 %all-to-all-done.1 = bf16[8,128,1024]{2,1,0:T(8,128)(2,1)} async-done(((bf16[8,128,1024]{2,1,0:T(8,128)(2,1)}), bf16[8,128,1024]{2,1,0:T(8,128)(2,1)}, u32[]{:S(2)}, u32[]{:S(2)}) %all-to-all-start.1) | async-done | bytes 2097184 | tf_op jit(solution)/shard_map/all_to_all | solution.py:139
  82.5 20.6 %all-gather.2.cloned.1.call-done = bf16[2,1024,1152]{2,1,0:T(8,128)(2,1)} async-done(((bf16[2,256,1152]{2,1,0:T(8,128)(2,1)}), bf16[2,1024,1152]{2,1,0:T(8,128)(2,1)}) %all-gather.2.cloned.1.call-update) | async-done | bytes 4718608 | tf_op jit(solution)/shard_map/all_gather | solution.py:151
  103.1 3.0 %fusion.35 = f32[384,1024]{1,0:T(8,128)S(1)} fusion(bf16[1024,1024]{1,0:T(8,128)(2,1)} %bitcast.6, bf16[2,1024,1152]{2,1,0:T(8,128)(2,1)} %all-gather.2.cloned.1.call-done), kind=kOutput, calls=%fused_computation.69 | convolution fusion | flops 805306368 | bytes 4456448 | tf_op jit(solution)/shard_map/dot_general | solution.py:132
  106.3 2.8 %fusion.36 = f32[384,1024]{1,0:T(8,128)S(1)} fusion(bf16[1024,1024]{1,0:T(8,128)(2,1)} %bitcast.6, bf16[2,1024,1152]{2,1,0:T(8,128)(2,1)S(1)} %copy-done), kind=kOutput, calls=%fused_computation.70 | convolution fusion | flops 805306368 | bytes 4456448 | tf_op jit(solution)/shard_map/dot_general | solution.py:132
  109.1 1.6 multiply_convert_fusion
  110.7 3.1 %fusion.22 = bf16[1,1024,384]{1,2,0:T(8,128)(2,1)S(1)} fusion(bf16[1024,384]{0,1:T(8,128)(2,1)S(1)} %get-tuple-element.17, bf16[1024,1024]{1,0:T(8,128)(2,1)} %bitcast.6), kind=kOutput, calls=%fused_computation.49 | convolution fusion | flops 805699584 | bytes 3670016 | tf_op jit(solution)/shard_map/dot_general | solution.py:132
  113.9 2.6 %fusion.23 = bf16[1,1024,384]{1,2,0:T(8,128)(2,1)S(1)} fusion(bf16[1024,384]{0,1:T(8,128)(2,1)S(1)} %get-tuple-element.16, bf16[1024,1024]{1,0:T(8,128)(2,1)} %bitcast.6), kind=kOutput, calls=%fused_computation.50 | convolution fusion | flops 805699584 | bytes 3670016 | tf_op jit(solution)/shard_map/dot_general | solution.py:132
  116.5 2.6 %fusion.30 = f32[384,1024]{1,0:T(8,128)S(1)} fusion(bf16[1024,1024]{1,0:T(8,128)(2,1)} %bitcast.6, bf16[2,1024,1152]{2,1,0:T(8,128)(2,1)S(1)} %copy-done), kind=kOutput, calls=%fused_computation.64 | convolution fusion | flops 805306368 | bytes 4456448 | tf_op jit(solution)/shard_map/dot_general | solution.py:132
  119.1 2.8 %fusion.32 = f32[384,1024]{1,0:T(8,128)S(1)} fusion(bf16[1024,1024]{1,0:T(8,128)(2,1)} %bitcast.6, bf16[2,1024,1152]{2,1,0:T(8,128)(2,1)S(1)} %copy-done), kind=kOutput, calls=%fused_computation.66 | convolution fusion | flops 805306368 | bytes 4456448 | tf_op jit(solution)/shard_map/dot_general | solution.py:132
  121.9 1.6 multiply_convert_fusion.1
  123.6 2.9 %fusion.20 = bf16[1,1024,384]{1,2,0:T(8,128)(2,1)S(1)} fusion(bf16[1024,384]{0,1:T(8,128)(2,1)S(1)} %get-tuple-element.20, bf16[1024,1024]{1,0:T(8,128)(2,1)} %bitcast.6), kind=kOutput, calls=%fused_computation.47 | convolution fusion | flops 805699584 | bytes 3670016 | tf_op jit(solution)/shard_map/dot_general | solution.py:132
  126.5 2.7 %fusion.21 = bf16[1,1024,384]{1,2,0:T(8,128)(2,1)S(1)} fusion(bf16[1024,384]{0,1:T(8,128)(2,1)S(1)} %get-tuple-element.19, bf16[1024,1024]{1,0:T(8,128)(2,1)} %bitcast.6), kind=kOutput, calls=%fused_computation.48 | convolution fusion | flops 805699584 | bytes 3670016 | tf_op jit(solution)/shard_map/dot_general | solution.py:132
  131.8 7.1 %maximum_maximum_fusion = bf16[2,1024,1152]{1,2,0:T(8,128)(2,1)} fusion(bf16[1,1024,384]{1,2,0:T(8,128)(2,1)S(1)} %fusion.25, bf16[1,1024,384]{1,2,0:T(8,128)(2,1)S(1)} %fusion.23, bf16[1,1024,384]{1,2,0:T(8,128)(2,1)S(1)} %fusion.22, bf16[1,1024,384]{1,2,0:T(8,128)(2,1)S(1)} %fusion.24, bf16[1,1024,384]{1,2,0:T(8,128)(2,1)S(1)} %fusion.21, ...), kind=kLoop, calls=%fused_computation | loop fusion | flops 28311552 | bytes 9437184 | tf_op jit(solution)/shard_map/stack | solution.py:178
  139.0 2.6 %fusion.34 = f32[1024,1024]{1,0:T(8,128)S(1)} fusion(bf16[1024,384]{0,1:T(8,128)(2,1)S(1)} %get-tuple-element.17, bf16[2,1024,1152]{2,1,0:T(8,128)(2,1)} %all-gather.2.cloned.1.call-done), kind=kOutput, calls=%fused_computation.68 | convolution fusion | flops 805306368 | bytes 5767168 | tf_op jit(solution)/shard_map/dot_general | solution.py:132
  141.7 1.3 fusion.29
  143.1 1.3 fusion.31
  144.4 2.8 %add_convert_fusion = bf16[1024,1024]{1,0:T(8,128)(2,1)} fusion(f32[1024,1024]{1,0:T(8,128)S(1)} %fusion.34, f32[1024,1024]{1,0:T(8,128)S(1)} %fusion.29, f32[1024,1024]{1,0:T(8,128)S(1)} %fusion.31, bf16[1024,384]{0,1:T(8,128)(2,1)S(1)} %copy-done.9, bf16[2,1024,1152]{2,1,0:T(8,128)(2,1)S(1)} %bitcast.161), kind=kOutput, calls=%fused_computation.9 | convolution fusion | flops 809500672 | bytes 16252928 | tf_op jit(solution)/shard_map/dot_general | solution.py:132
  147.3 3.7 %all-to-all-start.4 = ((bf16[8,128,1024]{2,1,0:T(8,128)(2,1)}), bf16[8,128,1024]{2,1,0:T(8,128)(2,1)S(1)}, u32[]{:S(2)}, u32[]{:S(2)}) async-start(bf16[8,128,1024]{2,1,0:T(8,128)(2,1)} %bitcast.159), calls=%async_computation.4 | async-start | bytes 4194304 | tf_op jit(solution)/shard_map/all_to_all | solution.py:184
  150.9 2.5 %fusion.26 = f32[1024,1024]{1,0:T(8,128)S(1)} fusion(bf16[1024,384]{0,1:T(8,128)(2,1)S(1)} %get-tuple-element.21, f32[1024]{0:T(1024)S(1)} %bitcast.167, bf16[2,1024,1152]{2,1,0:T(8,128)(2,1)} %all-gather.2.cloned.1.call-done), kind=kOutput, calls=%fused_computation.54 | convolution fusion | flops 806486016 | bytes 5771264 | tf_op jit(solution)/shard_map/dot_general | solution.py:132
  153.4 3.8 %add_convert_fusion.1 = bf16[1024,1024]{1,0:T(8,128)(2,1)} fusion(f32[1024,1024]{1,0:T(8,128)S(1)} %fusion.26, bf16[1024,384]{0,1:T(8,128)(2,1)S(1)} %copy-done.11, f32[1024]{0:T(1024)S(1)} %bitcast.170, bf16[2,1024,1152]{2,1,0:T(8,128)(2,1)} %all-gather.2.cloned.1.call-done), kind=kOutput, calls=%fused_computation.10 | convolution fusion | flops 808583168 | bytes 7868416 | tf_op jit(solution)/shard_map/dot_general | solution.py:132
  157.2 20.3 %all-to-all-done.4 = bf16[8,128,1024]{2,1,0:T(8,128)(2,1)S(1)} async-done(((bf16[8,128,1024]{2,1,0:T(8,128)(2,1)}), bf16[8,128,1024]{2,1,0:T(8,128)(2,1)S(1)}, u32[]{:S(2)}, u32[]{:S(2)}) %all-to-all-start.4) | async-done | bytes 2097184 | tf_op jit(solution)/shard_map/all_to_all | solution.py:184
  177.5 4.3 %all-to-all-start.2 = ((bf16[8,128,1024]{2,1,0:T(8,128)(2,1)}), bf16[8,128,1024]{2,1,0:T(8,128)(2,1)}, u32[]{:S(2)}, u32[]{:S(2)}) async-start(bf16[8,128,1024]{2,1,0:T(8,128)(2,1)} %bitcast.17), calls=%async_computation.2 | async-start | bytes 4194304 | tf_op jit(solution)/shard_map/all_to_all | solution.py:184
  183.0 25.5 %all-to-all-done.2 = bf16[8,128,1024]{2,1,0:T(8,128)(2,1)} async-done(((bf16[8,128,1024]{2,1,0:T(8,128)(2,1)}), bf16[8,128,1024]{2,1,0:T(8,128)(2,1)}, u32[]{:S(2)}, u32[]{:S(2)}) %all-to-all-start.2) | async-done | bytes 2097184 | tf_op jit(solution)/shard_map/all_to_all | solution.py:184
  208.5 2.7 %reduce_sum.34 = bf16[128,1024]{1,0:T(8,128)(2,1)} reduce(bf16[8,128,1024]{2,1,0:T(8,128)(2,1)} %all-to-all-done.2, bf16[]{:T(256)} %constant.6.clone.1), dimensions={0}, to_apply=%region_1.2 | reduce | flops 917504 | bytes 2359298 | tf_op jit(solution)/shard_map/reduce_sum | solution.py:185
  211.2 11.6 %reduce-scatter.2.cloned.1.call-done = bf16[2,256,1152]{1,2,0:T(8,128)(2,1)} async-done(((bf16[2,1024,1152]{1,2,0:T(8,128)(2,1)}), bf16[2,256,1152]{1,2,0:T(8,128)(2,1)}) %reduce-scatter.2.cloned.1.call-update) | async-done | bytes 1179664 | tf_op jit(solution)/shard_map/reduce_scatter | solution.py:178
  (52 shorter events, 8.8 us)
Async XLA Ops:
  7.2 95.9 %all-gather.2.cloned.1.call-start = ((), (), s32[]{:S(2)}) async-start(), calls=%async_computation.6 | async-start | bytes 5898240 | tf_op jit(solution)/shard_map/all_gather | solution.py:151
  7.2 3.6 %copy-start.14 = (f32[128,8]{0,1:T(8,128)S(1)}, f32[128,8]{0,1:T(8,128)}, u32[]{:S(2)}) copy-start(f32[128,8]{0,1:T(8,128)} %param.8) | copy-start | bytes 12292
  7.2 3.6 %copy-start.15 = (s32[128,8]{0,1:T(8,128)S(1)}, s32[128,8]{0,1:T(8,128)}, u32[]{:S(2)}) copy-start(s32[128,8]{0,1:T(8,128)} %param.7) | copy-start | bytes 12292
  7.2 13.3 %copy-start.12 = (bf16[128,1024]{1,0:T(8,128)(2,1)S(1)}, bf16[128,1024]{1,0:T(8,128)(2,1)}, u32[]{:S(2)}) copy-start(bf16[128,1024]{1,0:T(8,128)(2,1)} %param.11) | copy-start | bytes 786436
  20.8 29.2 %copy-start.13 = (bf16[128,1024]{1,0:T(8,128)(2,1)S(1)}, bf16[128,1024]{1,0:T(8,128)(2,1)}, u32[]{:S(2)}) copy-start(bf16[128,1024]{1,0:T(8,128)(2,1)} %param.6) | copy-start | bytes 786436
  51.5 31.0 %all-to-all-start.1 = ((bf16[8,128,1024]{2,1,0:T(8,128)(2,1)}), bf16[8,128,1024]{2,1,0:T(8,128)(2,1)}, u32[]{:S(2)}, u32[]{:S(2)}) async-start(bf16[8,128,1024]{2,1,0:T(8,128)(2,1)} %broadcast_in_dim.18), calls=%async_computation.1 | async-start | bytes 4194304 | tf_op jit(solution)/shard_map/all_to_all | solution.py:139
  55.9 166.9 %reduce-scatter.2.cloned.1.call-start = ((), (), s32[]{:S(2)}) async-start(), calls=%async_computation.7 | async-start | bytes 5898240 | tf_op jit(solution)/shard_map/reduce_scatter | solution.py:178
  103.1 3.2 %copy-start = (bf16[2,1024,1152]{2,1,0:T(8,128)(2,1)S(1)}, bf16[2,1024,1152]{2,1,0:T(8,128)(2,1)}, u32[]{:S(2)}) copy-start(bf16[2,1024,1152]{2,1,0:T(8,128)(2,1)} %all-gather.2.cloned.1.call-done) | copy-start | bytes 14155780
  106.3 2.8 %copy-start.7 = (bf16[8,128,1024]{2,1,0:T(8,128)(2,1)S(1)}, bf16[8,128,1024]{2,1,0:T(8,128)(2,1)}, u32[]{:S(2)}) copy-start(bf16[8,128,1024]{2,1,0:T(8,128)(2,1)} %get-tuple-element.25) | copy-start | bytes 6291460
  110.7 3.2 %copy-start.8 = (bf16[1024,384]{0,1:T(8,128)(2,1)}, bf16[1024,384]{0,1:T(8,128)(2,1)S(1)}, u32[]{:S(2)}) copy-start(bf16[1024,384]{0,1:T(8,128)(2,1)S(1)} %get-tuple-element.16) | copy-start | bytes 2359300
  110.7 18.5 %copy-start.10 = (bf16[1024,384]{0,1:T(8,128)(2,1)}, bf16[1024,384]{0,1:T(8,128)(2,1)S(1)}, u32[]{:S(2)}) copy-start(bf16[1024,384]{0,1:T(8,128)(2,1)S(1)} %get-tuple-element.18) | copy-start | bytes 2359300
  119.1 2.8 %copy-start.6 = (bf16[8,128,1024]{2,1,0:T(8,128)(2,1)S(1)}, bf16[8,128,1024]{2,1,0:T(8,128)(2,1)}, u32[]{:S(2)}) copy-start(bf16[8,128,1024]{2,1,0:T(8,128)(2,1)} %get-tuple-element.24) | copy-start | bytes 6291460
  123.6 2.9 %copy-start.2 = (bf16[1024,384]{0,1:T(8,128)(2,1)}, bf16[1024,384]{0,1:T(8,128)(2,1)S(1)}, u32[]{:S(2)}) copy-start(bf16[1024,384]{0,1:T(8,128)(2,1)S(1)} %get-tuple-element.20) | copy-start | bytes 2359300
  126.5 2.7 %copy-start.5 = (bf16[1024,1024]{1,0:T(8,128)(2,1)S(1)}, bf16[1024,1024]{1,0:T(8,128)(2,1)}, u32[]{:S(2)}) copy-start(bf16[1024,1024]{1,0:T(8,128)(2,1)} %get-tuple-element.23) | copy-start | bytes 6291460
  129.2 1.6 copy-start.4
  138.9 2.6 %slice-start = ((s8[4718592]{0:T(1024)(128)(4,1)}), s8[524288]{0:T(1024)(128)(4,1)S(1)}, s32[]{:S(2)}) async-start(s8[4718592]{0:T(1024)(128)(4,1)} %bitcast.160), calls=%async_computation.8 | async-start | bytes 1048576
  139.0 2.6 %slice-start.1 = ((s8[4718592]{0:T(1024)(128)(4,1)}), s8[4194304]{0:T(1024)(128)(4,1)S(1)}, s32[]{:S(2)}) async-start(s8[4718592]{0:T(1024)(128)(4,1)} %bitcast.160), calls=%async_computation.9 | async-start | bytes 8388608
  139.0 2.8 %copy-start.3 = (bf16[1024,384]{0,1:T(8,128)(2,1)S(1)}, bf16[1024,384]{0,1:T(8,128)(2,1)}, u32[]{:S(2)}) copy-start(bf16[1024,384]{0,1:T(8,128)(2,1)} %copy-done.2) | copy-start | bytes 2359300
  143.1 1.4 copy-start.9
  147.3 30.3 %all-to-all-start.4 = ((bf16[8,128,1024]{2,1,0:T(8,128)(2,1)}), bf16[8,128,1024]{2,1,0:T(8,128)(2,1)S(1)}, u32[]{:S(2)}, u32[]{:S(2)}) async-start(bf16[8,128,1024]{2,1,0:T(8,128)(2,1)} %bitcast.159), calls=%async_computation.4 | async-start | bytes 4194304 | tf_op jit(solution)/shard_map/all_to_all | solution.py:184
  150.9 2.5 %copy-start.11 = (bf16[1024,384]{0,1:T(8,128)(2,1)S(1)}, bf16[1024,384]{0,1:T(8,128)(2,1)}, u32[]{:S(2)}) copy-start(bf16[1024,384]{0,1:T(8,128)(2,1)} %copy-done.10) | copy-start | bytes 2359300
  177.5 31.0 %all-to-all-start.2 = ((bf16[8,128,1024]{2,1,0:T(8,128)(2,1)}), bf16[8,128,1024]{2,1,0:T(8,128)(2,1)}, u32[]{:S(2)}, u32[]{:S(2)}) async-start(bf16[8,128,1024]{2,1,0:T(8,128)(2,1)} %bitcast.17), calls=%async_computation.2 | async-start | bytes 4194304 | tf_op jit(solution)/shard_map/all_to_all | solution.py:184
  222.8 1.1 slice-start.2
  222.8 2.3 copy-start.1
Sparse Core Ops, SparseCore 0:
  10.9 92.0 all-gather.1
  139.1 83.6 reduce-scatter.1

commit v2 on v0

--- a/solution.py
+++ b/solution.py
@@ -1,6 +1,10 @@
+import functools
+
 import jax
 import jax.numpy as jnp
 from jax import lax
+from jax.experimental import pallas as pl
+from jax.experimental.pallas import tpu as pltpu
 from jax.sharding import PartitionSpec as P
 
 
@@ -14,7 +18,7 @@
     return flat_back[target].reshape(tok_rows, top_count, returned.shape[-1])
 
 
-def shards(tokens, expert_ids, combine_weights, lift_weights, down_weights, cotangent):
+def slot_shards(tokens, expert_ids, combine_weights, lift_weights, down_weights, cotangent):
     tok_rows, top_count = expert_ids.shape
     local_experts = lift_weights.shape[0]
     hidden_width = down_weights.shape[1]
@@ -128,6 +132,412 @@
     return (layer_output, token_grads, lift_grads, down_grads)
 
 
+MESH = pl.DeviceIdType.MESH
+
+
+def dot(left, right, left_dim, right_dim):
+    return lax.dot_general(
+        left, right, (((left_dim,), (right_dim,)), ((), ())), preferred_element_type=jnp.float32
+    )
+
+
+def fused(owners, planes, per_expert, *refs):
+    (tok_in, cot_in, gate_in, packed, part_out, layer_out, grad_out) = refs[:7]
+    (weights, parts, from_left, from_right) = refs[7:11]
+    (tok_all, cot_all, gate_all, tok_flip, cot_flip) = refs[11:16]
+    (weighted, hidden_grads, totals, paired_in, paired, chip_in) = refs[16:22]
+    (own_sem, w_send, w_recv, p_send, p_recv) = refs[22:27]
+    (direct_send, direct_recv, pass_send, pass_recv) = refs[27:31]
+    (pair_send, pair_recv, chip_send, chip_recv) = refs[31:35]
+    stages, slice_rows, packed_width = packed.shape
+    width = packed_width // 3
+    tok_rows, model_width = tok_in.shape
+    hops = planes - 1
+    chips = owners // 2
+    e, z = lax.axis_index("expert"), lax.axis_index("dp")
+    chip, core = e // 2, e % 2
+    partner = chip * 2 + 1 - core
+    experts = stages // per_expert
+
+    def at(device, plane):
+        return (device, plane)
+
+    def chip_at(delta):
+        return lax.rem(chip + delta, chips)
+
+    barrier = pltpu.get_barrier_semaphore()
+    for delta in range(1, chips):
+        pl.semaphore_signal(
+            barrier, inc=1, device_id=at(chip_at(delta) * 2 + core, z), device_id_type=MESH
+        )
+    pl.semaphore_signal(barrier, inc=1, device_id=at(partner, z), device_id_type=MESH)
+
+    @pl.when(z > 0)
+    def _():
+        pl.semaphore_signal(barrier, inc=1, device_id=at(e, z - 1), device_id_type=MESH)
+
+    @pl.when(z < planes - 1)
+    def _():
+        pl.semaphore_signal(barrier, inc=1, device_id=at(e, z + 1), device_id_type=MESH)
+
+    end = (z == 0) | (z == planes - 1)
+
+    @pl.when(end)
+    def _():
+        pl.semaphore_wait(barrier, chips + 1)
+
+    @pl.when(jnp.logical_not(end))
+    def _():
+        pl.semaphore_wait(barrier, chips + 2)
+
+    def remote(src, dst, send, recv, device):
+        return pltpu.make_async_remote_copy(
+            src_ref=src, dst_ref=dst, send_sem=send, recv_sem=recv,
+            device_id=device, device_id_type=MESH,
+        )
+
+    arrays = ((tok_in, tok_all), (cot_in, cot_all), (gate_in, gate_all))
+
+    def own_copies():
+        copies = [
+            pltpu.make_async_copy(source, full.at[e], own_sem.at[i])
+            for i, (source, full) in enumerate(arrays)
+        ]
+        return copies + [
+            pltpu.make_async_copy(packed.at[s], weights.at[s, z], own_sem.at[len(arrays) + s])
+            for s in range(stages)
+        ]
+
+    def direct(i, delta):
+        source, full = arrays[i]
+        return remote(
+            source, full.at[e], direct_send.at[i, delta], direct_recv.at[i, delta],
+            at(chip_at(delta) * 2 + core, z),
+        )
+
+    def passed(i, delta):
+        source, full = arrays[i]
+        origin = chip_at(chips - delta) * 2 + core
+        return remote(
+            source if delta == 0 else full.at[origin], full.at[e if delta == 0 else origin],
+            pass_send.at[i, delta], pass_recv.at[i, delta], at(partner, z),
+        )
+
+    kinds = range(len(arrays))
+    for copy in own_copies():
+        copy.start()
+    for i in kinds:
+        for delta in range(1, chips):
+            direct(i, delta).start()
+        passed(i, 0).start()
+
+    def gather(way, hop, s):
+        origin = z - hop if way == 0 else z + hop
+        source = packed.at[s] if hop == 0 else weights.at[s, origin]
+        return remote(
+            source, weights.at[s, origin], w_send.at[way, hop], w_recv.at[way, hop, s],
+            at(e, z + 1 if way == 0 else z - 1),
+        )
+
+    def gather_sends(way, hop):
+        if way == 0:
+            return (z >= hop) & (z < planes - 1)
+        return (z + hop <= planes - 1) & (z > 0)
+
+    def gather_takes(way, hop):
+        return z >= hop + 1 if way == 0 else z + hop + 1 <= planes - 1
+
+    def arrived(way, hop, s):
+        origin = z - 1 - hop if way == 0 else z + 1 + hop
+        landed = weights.at[s, origin]
+        return remote(landed, landed, w_send.at[way, hop], w_recv.at[way, hop, s], at(e, z))
+
+    def reduce(way, hop, s):
+        if way == 0:
+            span, full, device = pl.ds(hop + 1, planes - 1 - hop), from_left, z + 1
+        else:
+            span, full, device = pl.ds(0, planes - 1 - hop), from_right, z - 1
+        return remote(
+            parts.at[s, span], full.at[s, span], p_send.at[way], p_recv.at[way, s], at(e, device)
+        )
+
+    def reducer(way, hop):
+        return hop if way == 0 else planes - 1 - hop
+
+    def compute(s):
+        expert = e * experts + s // per_expert
+
+        def forward(i, carry):
+            pair = pl.ds(i * 2, 2)
+            rows = tok_all[pair].reshape(2 * tok_rows, model_width)
+            back = cot_all[pair].reshape(2 * tok_rows, model_width)
+            gates = gate_all[pair].reshape(2 * tok_rows, gate_in.shape[1])
+            lane = lax.broadcasted_iota(jnp.int32, gates.shape, 1)
+            gate = jnp.sum(jnp.where(lane == expert, gates, 0.0), axis=1, keepdims=True)
+            whole = weights[s].reshape(model_width, packed_width)
+            hidden = dot(rows, whole[:, : 2 * width], 1, 0)
+            act_grad = dot(back, whole[:, 2 * width :], 1, 0) * gate
+            gate_term, up_term = hidden[:, :width], hidden[:, width:]
+            sigmoid_val = 1.0 / (1.0 + jnp.exp(-gate_term))
+            swished = gate_term * sigmoid_val
+            slopes = sigmoid_val * (1.0 + gate_term * (1.0 - sigmoid_val))
+            place = pl.ds(i * 2 * tok_rows, 2 * tok_rows)
+            weighted[s, place, :] = (swished * up_term * gate).astype(jnp.bfloat16)
+            hidden_grads[s, place, :width] = (act_grad * up_term * slopes).astype(jnp.bfloat16)
+            hidden_grads[s, place, width:] = (act_grad * swished).astype(jnp.bfloat16)
+            return carry
+
+        lax.fori_loop(0, chips, forward, 0)
+
+        def backward(d, carry):
+            parts[s, d, :, : 2 * width] = dot(tok_flip[d], hidden_grads[s], 1, 0).astype(
+                jnp.bfloat16
+            )
+            parts[s, d, :, 2 * width :] = dot(cot_flip[d], weighted[s], 1, 0).astype(jnp.bfloat16)
+            return carry
+
+        lax.fori_loop(0, planes, backward, 0)
+
+    def pair_copy(a, q):
+        return remote(
+            totals.at[a, q * 2 + 1 - core], paired_in.at[a, q],
+            pair_send.at[a, q], pair_recv.at[a, q], at(partner, z),
+        )
+
+    def chip_copy(a, delta):
+        return remote(
+            paired.at[a, chip_at(delta)], chip_in.at[a, delta],
+            chip_send.at[a, delta], chip_recv.at[a, delta], at(chip_at(delta) * 2 + core, z),
+        )
+
+    def finish_rows():
+        def rows_of(i, carry):
+            place = pl.ds(i * 2 * tok_rows, 2 * tok_rows)
+            for o in range(planes):
+                columns = slice(o * slice_rows, (o + 1) * slice_rows)
+                outs = grads = 0.0
+                for s in range(stages):
+                    outs += dot(weighted[s, place, :], weights[s, o, :, 2 * width :], 1, 1)
+                    grads += dot(hidden_grads[s, place, :], weights[s, o, :, : 2 * width], 1, 1)
+                shape = (2, tok_rows, slice_rows)
+                totals[0, pl.ds(i * 2, 2), :, columns] = outs.astype(jnp.bfloat16).reshape(shape)
+                totals[1, pl.ds(i * 2, 2), :, columns] = grads.astype(jnp.bfloat16).reshape(shape)
+            return carry
+
+        lax.fori_loop(0, chips, rows_of, 0)
+
+    def step(k, carry):
+        for way in range(2):
+            for hop in range(hops):
+                s = k - 1 - hop
+                live = (s >= 0) & (s < stages)
+
+                @pl.when(live & gather_takes(way, hop))
+                def _():
+                    arrived(way, hop, s).wait_recv()
+
+                @pl.when(live & gather_sends(way, hop))
+                def _():
+                    gather(way, hop, s).wait_send()
+
+        for way in range(2):
+            for hop in range(hops):
+                s = k - 1 - (hops + 1) - hop
+                live = (s >= 0) & (s < stages)
+
+                @pl.when(live & (z == reducer(way, hop)))
+                def _():
+                    reduce(way, hop, s).wait_send()
+
+                @pl.when(live & (z == reducer(way, hop + 1)))
+                def _():
+                    reduce(way, hop, s).wait_recv()
+                    onward = planes - 2 - hop
+                    full = from_left if way == 0 else from_right
+                    for step_to in range(onward):
+                        d = hop + 2 + step_to if way == 0 else step_to
+                        parts[s, d] = (
+                            parts[s, d].astype(jnp.float32) + full[s, d].astype(jnp.float32)
+                        ).astype(jnp.bfloat16)
+
+        for way in range(2):
+            for hop in range(hops):
+                s = k - hop
+
+                @pl.when((s >= 0) & (s < stages) & gather_sends(way, hop))
+                def _():
+                    gather(way, hop, s).start()
+
+                t = k - (hops + 1) - hop
+
+                @pl.when((t >= 0) & (t < stages) & (z == reducer(way, hop)))
+                def _():
+                    reduce(way, hop, t).start()
+
+        @pl.when(k == hops - 1)
+        def _():
+            for i in kinds:
+                for delta in range(1, chips):
+                    direct(i, delta).wait_recv()
+                    passed(i, delta).start()
+
+        @pl.when(k == hops)
+        def _():
+            for copy in own_copies():
+                copy.wait()
+            for i in kinds:
+                for delta in range(chips):
+                    passed(i, delta).wait()
+                for delta in range(1, chips):
+                    direct(i, delta).wait_send()
+
+            def flip(j, carry):
+                for d in range(planes):
+                    columns = slice(d * slice_rows, (d + 1) * slice_rows)
+                    for full, flipped in ((tok_all, tok_flip), (cot_all, cot_flip)):
+                        block = full[j, :, columns].astype(jnp.float32)
+                        flipped[d, :, j * tok_rows : (j + 1) * tok_rows] = block.T.astype(
+                            jnp.bfloat16
+                        )
+                return carry
+
+            for j in range(owners):
+                flip(j, 0)
+
+        @pl.when((k >= hops) & (k < hops + stages))
+        def _():
+            compute(k - hops)
+
+        @pl.when(k == hops + stages)
+        def _():
+            finish_rows()
+            for a in range(2):
+                for q in range(chips):
+                    pair_copy(a, q).start()
+
+        @pl.when(k == hops + stages + 1)
+        def _():
+            for a in range(2):
+                for q in range(chips):
+                    pair_copy(a, q).wait()
+                    paired[a, q] = (
+                        totals[a, q * 2 + core].astype(jnp.float32)
+                        + paired_in[a, q].astype(jnp.float32)
+                    ).astype(jnp.bfloat16)
+            for a in range(2):
+                for delta in range(1, chips):
+                    chip_copy(a, delta).start()
+
+        s = k - (2 * hops + 1)
+
+        @pl.when((s >= 0) & (s < stages))
+        def _():
+            mine = parts[s, z].astype(jnp.float32)
+
+            @pl.when(z == 0)
+            def _():
+                part_out[s] = (mine + from_right[s, z].astype(jnp.float32)).astype(jnp.bfloat16)
+
+            @pl.when(z == planes - 1)
+            def _():
+                part_out[s] = (mine + from_left[s, z].astype(jnp.float32)).astype(jnp.bfloat16)
+
+            @pl.when((z > 0) & (z < planes - 1))
+            def _():
+                sides = from_left[s, z].astype(jnp.float32) + from_right[s, z].astype(jnp.float32)
+                part_out[s] = (mine + sides).astype(jnp.bfloat16)
+
+        return carry
+
+    lax.fori_loop(0, stages + 2 * hops + 1, step, 0)
+    for a, result in enumerate((layer_out, grad_out)):
+        total = paired[a, chip].astype(jnp.float32)
+        for delta in range(1, chips):
+            chip_copy(a, delta).wait()
+            total += chip_in[a, delta].astype(jnp.float32)
+        result[...] = total.astype(jnp.bfloat16)
+
+
+def dense_shards(tokens, expert_ids, combine_weights, lift_weights, down_weights, cotangent):
+    tok_rows, top_count = expert_ids.shape
+    experts, slice_rows, _ = lift_weights.shape
+    hidden_width = down_weights.shape[1]
+    model_width = tokens.shape[1]
+    owners, planes = lax.axis_size("expert"), lax.axis_size("dp")
+    chips = owners // 2
+    all_rows = owners * tok_rows
+    lanes = -(-owners * experts // 128) * 128
+    width = 128 if hidden_width % 128 == 0 else hidden_width
+    per_expert = hidden_width // width
+    stages = experts * per_expert
+    named = expert_ids[:, :, None] == jnp.arange(lanes, dtype=jnp.int32)[None, None, :]
+    gates = jnp.sum(jnp.where(named, combine_weights[:, :, None], 0.0), axis=1)
+    packed = jnp.concatenate(
+        [lift_weights, jnp.transpose(down_weights, (0, 2, 1))], axis=2
+    ).reshape(experts, slice_rows, 3, per_expert, width)
+    packed = jnp.transpose(packed, (0, 3, 1, 2, 4)).reshape(stages, slice_rows, 3 * width)
+    bf16, dma = jnp.bfloat16, pltpu.SemaphoreType.DMA
+    full = (stages, planes, slice_rows, 3 * width)
+    vmem = pl.BlockSpec(memory_space=pltpu.VMEM)
+    parts, layer_output, token_grads = pl.pallas_call(
+        functools.partial(fused, owners, planes, per_expert),
+        out_shape=(
+            jax.ShapeDtypeStruct(packed.shape, bf16),
+            jax.ShapeDtypeStruct(tokens.shape, bf16),
+            jax.ShapeDtypeStruct(tokens.shape, bf16),
+        ),
+        in_specs=[vmem] * 4,
+        out_specs=[vmem] * 3,
+        scratch_shapes=[
+            pltpu.VMEM(full, bf16),
+            pltpu.VMEM(full, bf16),
+            pltpu.VMEM(full, bf16),
+            pltpu.VMEM(full, bf16),
+            pltpu.VMEM((owners, tok_rows, model_width), bf16),
+            pltpu.VMEM((owners, tok_rows, model_width), bf16),
+            pltpu.VMEM((owners, tok_rows, lanes), jnp.float32),
+            pltpu.VMEM((planes, slice_rows, all_rows), bf16),
+            pltpu.VMEM((planes, slice_rows, all_rows), bf16),
+            pltpu.VMEM((stages, all_rows, width), bf16),
+            pltpu.VMEM((stages, all_rows, 2 * width), bf16),
+            pltpu.VMEM((2, owners, tok_rows, model_width), bf16),
+            pltpu.VMEM((2, chips, tok_rows, model_width), bf16),
+            pltpu.VMEM((2, chips, tok_rows, model_width), bf16),
+            pltpu.VMEM((2, chips, tok_rows, model_width), bf16),
+            dma((3 + stages,)),
+            dma((2, planes)),
+            dma((2, planes, stages)),
+            dma((2,)),
+            dma((2, stages)),
+            dma((3, chips)),
+            dma((3, chips)),
+            dma((3, chips)),
+            dma((3, chips)),
+            dma((2, chips)),
+            dma((2, chips)),
+            dma((2, chips)),
+            dma((2, chips)),
+        ],
+        compiler_params=pltpu.CompilerParams(
+            collective_id=0, has_side_effects=True, vmem_limit_bytes=60 * 1024 * 1024
+        ),
+    )(tokens, cotangent, gates, packed)
+    parts = parts.reshape(experts, per_expert, slice_rows, 3, width)
+    parts = jnp.transpose(parts, (0, 2, 3, 1, 4)).reshape(experts, slice_rows, 3 * hidden_width)
+    lift_grads = parts[:, :, : 2 * hidden_width]
+    down_grads = jnp.transpose(parts[:, :, 2 * hidden_width :], (0, 2, 1))
+    return (layer_output, token_grads, lift_grads, down_grads)
+
+
+def shards(tokens, expert_ids, combine_weights, lift_weights, down_weights, cotangent):
+    tok_rows, top_count = expert_ids.shape
+    local_experts = lift_weights.shape[0]
+    all_experts = local_experts * lax.axis_size("expert")
+    capacity = max(2, 3 * tok_rows * top_count // (2 * all_experts))
+    plan = dense_shards if tok_rows <= local_experts * capacity else slot_shards
+    return plan(tokens, expert_ids, combine_weights, lift_weights, down_weights, cotangent)
+
+
 def solution(mesh):
     in_specs = (
         P(("expert", "dp"), None),

time: 263 us -> 176 us (0.67)
  Pallas kernels: 0 us -> 164 us
  waiting for transfers between devices: 125 us -> 0 us
  local copies, waits for them, and re-layouts: 54.9 us -> 9.57 us
  matrix products: 27.3 us -> 0 us
  other arithmetic: 22.5 us -> 1.05 us
  starting transfers between devices: 18.4 us -> 0 us
  between operations: 14.1 us -> 0.71 us
    pallas_call x0 -> x1, Pallas kernels: none -> 164 us  [dense_shards(): pl.pallas_call(functools.partial(fused, owners, planes, per_expert), out_...]
    all_to_all x4 -> x0, waiting for transfers between devices: 123 us -> none  [the longest x1 34.6 us: shards(): lax.all_to_all(send_rows, 'expert', split_axis=1, concat_axis=1, tiled=True)]
    gather x5 -> x0, local copies, waits for them, and re-layouts: 27.5 us -> none  [the longest x2 10.7 us: collect(): return flat_back[target].reshape(tok_rows, top_count, returned.shape[-1])]
    dot_general x12 -> x0, matrix products: 27.3 us -> none  [the longest x1 5.34 us: shards(): jnp.einsum('erd,edf->erf', part_rows, portion[:, :, :hidden_width], prefe...]
    all_to_all x4 -> x0, starting transfers between devices: 18.1 us -> none  [the longest x1 5.33 us: shards(): lax.all_to_all(send_back, 'expert', split_axis=1, concat_axis=1, tiled=True)]
    all_to_all x4 -> x0, local copies, waits for them, and re-layouts: 9.34 us -> none  [the longest x1 2.37 us: shards(): lax.all_to_all(result.reshape(buffer_shape), 'expert', split_axis=1, conc...]
    another operation x5 -> x0, other arithmetic: 8.57 us -> none
    reduce_sum x3 -> x1, other arithmetic: 5.97 us -> 0.97 us  [dense_shards(): gates = jnp.sum(jnp.where(named, combine_weights[:, :, None], 0.0), axis=1)]
  transfers between devices with their start and end apart: 7 -> 0, of which waited for: 4 -> 0; matrix products, arithmetic and copies ran while one was open for 31% -> 0% of each run, Pallas kernels for 0% -> 0%
where the time goes in v2:
time: 176 us; the launch traced here: 175 us
  Pallas kernels  164 us (93%)
  local copies, waits for them, and re-layouts  9.57 us (5%)
    pallas_call x1, Pallas kernels, dense_shards(): pl.pallas_call(functools.partial(fused, owners, planes, per_expert), out_...  164 us
    unnamed x12, local copies, waits for them, and re-layouts  5.6 us

profile of v2, /device:TPU:0, one launch (start us, length us, event | category | flops | bytes accessed | tf_op | source)
XLA Modules:
  0.0 175.4 jit_solution(6270460368766850519)
XLA Ops:
  0.6 0.0 copy-start
  0.6 0.8 copy.31
  1.5 0.8 copy.32
  2.3 1.0 select_reduce_fusion.refs_2_
  3.2 1.4 copy.33
  4.6 0.0 copy-done
  4.7 0.1 pad_maximum_fusion
  4.7 0.1 copy.34
  4.8 1.4 copy.35.refs_3_
  6.3 164.0 %shard_map.93 = (bf16[6,256,384]{2,1,0:T(8,128)(2,1)}, bf16[128,1024]{1,0:T(8,128)(2,1)}, bf16[128,1024]{1,0:T(8,128)(2,1)}) custom-call(bf16[128,1024]{1,0:T(8,128)(2,1)} %refs_0_.1, bf16[128,1024]{1,0:T(8,128)(2,1)} %refs_1_.1, f32[128,128]{1,0:T(8,128)} %select_reduce_fusion.refs_2_, bf16[6,256,384]{2,1,0:T(8,128)(2,1)} %copy.35.refs_3_), custom_call_target="tpu_custom_call" | custom-call | tf_op jit(solution)/shard_map/pallas_call | solution.py:482
  170.3 1.6 copy.36
  171.9 0.1 copy.37
  172.0 0.8 slice_bitcast_fusion
  172.7 0.1 slice.8
  172.8 0.0 copy-start.2
  172.8 0.0 copy-start.1
  172.8 1.2 copy.38
  174.0 0.0 copy-done.2
  174.0 0.7 copy.41
  174.7 0.0 copy-done.1
  174.7 0.7 copy.42
Async XLA Ops:
  0.6 4.0 %copy-start = (bf16[2,384,256]{2,1,0:T(8,128)(2,1)S(1)}, bf16[2,384,256]{2,1,0:T(8,128)(2,1)}, u32[]{:S(2)}) copy-start(bf16[2,384,256]{2,1,0:T(8,128)(2,1)} %param.10) | copy-start | bytes 1179652
  172.8 1.2 copy-start.2
  172.8 1.9 %copy-start.1 = (bf16[128,1024]{1,0:T(8,128)(2,1)S(1)}, bf16[128,1024]{1,0:T(8,128)(2,1)}, u32[]{:S(2)}) copy-start(bf16[128,1024]{1,0:T(8,128)(2,1)} %get-tuple-element.31) | copy-start | bytes 786436

commit v3 on v2

--- a/solution.py
+++ b/solution.py
@@ -142,13 +142,13 @@
 
 
 def fused(owners, planes, per_expert, *refs):
-    (tok_in, cot_in, gate_in, packed, part_out, layer_out, grad_out) = refs[:7]
-    (weights, parts, from_left, from_right) = refs[7:11]
-    (tok_all, cot_all, gate_all, tok_flip, cot_flip) = refs[11:16]
-    (weighted, hidden_grads, totals, paired_in, paired, chip_in) = refs[16:22]
-    (own_sem, w_send, w_recv, p_send, p_recv) = refs[22:27]
-    (direct_send, direct_recv, pass_send, pass_recv) = refs[27:31]
-    (pair_send, pair_recv, chip_send, chip_recv) = refs[31:35]
+    (tok_in, cot_in, gate_in, packed, lift_out, down_out, layer_out, grad_out) = refs[:8]
+    (weights, parts, from_left, from_right) = refs[8:12]
+    (tok_all, cot_all, gate_all, tok_flip, cot_flip) = refs[12:17]
+    (weighted, hidden_grads, totals, paired_in, paired, chip_in) = refs[17:23]
+    (own_sem, w_send, w_recv, p_send, p_recv) = refs[23:28]
+    (direct_send, direct_recv, pass_send, pass_recv) = refs[28:32]
+    (pair_send, pair_recv, chip_send, chip_recv) = refs[32:36]
     stages, slice_rows, packed_width = packed.shape
     width = packed_width // 3
     tok_rows, model_width = tok_in.shape
@@ -235,7 +235,7 @@
         origin = z - hop if way == 0 else z + hop
         source = packed.at[s] if hop == 0 else weights.at[s, origin]
         return remote(
-            source, weights.at[s, origin], w_send.at[way, hop], w_recv.at[way, hop, s],
+            source, weights.at[s, origin], w_send.at[way, hop, s], w_recv.at[way, hop, s],
             at(e, z + 1 if way == 0 else z - 1),
         )
 
@@ -250,7 +250,7 @@
     def arrived(way, hop, s):
         origin = z - 1 - hop if way == 0 else z + 1 + hop
         landed = weights.at[s, origin]
-        return remote(landed, landed, w_send.at[way, hop], w_recv.at[way, hop, s], at(e, z))
+        return remote(landed, landed, w_send.at[way, hop, s], w_recv.at[way, hop, s], at(e, z))
 
     def reduce(way, hop, s):
         if way == 0:
@@ -258,7 +258,7 @@
         else:
             span, full, device = pl.ds(0, planes - 1 - hop), from_right, z - 1
         return remote(
-            parts.at[s, span], full.at[s, span], p_send.at[way], p_recv.at[way, s], at(e, device)
+            parts.at[s, span], full.at[s, span], p_send.at[way, s], p_recv.at[way, s], at(e, device)
         )
 
     def reducer(way, hop):
@@ -341,6 +341,14 @@
                     gather(way, hop, s).wait_send()
 
         for way in range(2):
+            for hop in range(hops - 1, -1, -1):
+                s = k - hop if hop else k + 1
+
+                @pl.when((s >= 0) & (s < stages) & gather_sends(way, hop))
+                def _():
+                    gather(way, hop, s).start()
+
+        for way in range(2):
             for hop in range(hops):
                 s = k - 1 - (hops + 1) - hop
                 live = (s >= 0) & (s < stages)
@@ -361,13 +369,7 @@
                         ).astype(jnp.bfloat16)
 
         for way in range(2):
-            for hop in range(hops):
-                s = k - hop
-
-                @pl.when((s >= 0) & (s < stages) & gather_sends(way, hop))
-                def _():
-                    gather(way, hop, s).start()
-
+            for hop in range(1, hops):
                 t = k - (hops + 1) - hop
 
                 @pl.when((t >= 0) & (t < stages) & (z == reducer(way, hop)))
@@ -404,18 +406,7 @@
             for j in range(owners):
                 flip(j, 0)
 
-        @pl.when((k >= hops) & (k < hops + stages))
-        def _():
-            compute(k - hops)
-
         @pl.when(k == hops + stages)
-        def _():
-            finish_rows()
-            for a in range(2):
-                for q in range(chips):
-                    pair_copy(a, q).start()
-
-        @pl.when(k == hops + stages + 1)
         def _():
             for a in range(2):
                 for q in range(chips):
@@ -428,26 +419,60 @@
                 for delta in range(1, chips):
                     chip_copy(a, delta).start()
 
+        @pl.when((k >= hops) & (k < hops + stages))
+        def _():
+            compute(k - hops)
+            for way in range(2):
+
+                @pl.when(z == reducer(way, 0))
+                def _():
+                    reduce(way, 0, k - hops).start()
+
+        @pl.when(k == hops + stages - 1)
+        def _():
+            finish_rows()
+            for a in range(2):
+                for q in range(chips):
+                    pair_copy(a, q).start()
+
         s = k - (2 * hops + 1)
 
         @pl.when((s >= 0) & (s < stages))
         def _():
             mine = parts[s, z].astype(jnp.float32)
+
+            def store(total):
+                owned, chunk = lax.div(s, per_expert), lax.rem(s, per_expert)
+                gate_at = pl.multiple_of(chunk * width, width)
+                up_at = pl.multiple_of((chunk + per_expert) * width, width)
+                lift_out[owned, :, pl.ds(gate_at, width)] = total[:, :width].astype(jnp.bfloat16)
+                lift_out[owned, :, pl.ds(up_at, width)] = total[:, width : 2 * width].astype(
+                    jnp.bfloat16
+                )
+                down_out[owned, pl.ds(gate_at, width), :] = total[:, 2 * width :].T.astype(
+                    jnp.bfloat16
+                )
 
             @pl.when(z == 0)
             def _():
-                part_out[s] = (mine + from_right[s, z].astype(jnp.float32)).astype(jnp.bfloat16)
+                store(mine + from_right[s, z].astype(jnp.float32))
 
             @pl.when(z == planes - 1)
             def _():
-                part_out[s] = (mine + from_left[s, z].astype(jnp.float32)).astype(jnp.bfloat16)
+                store(mine + from_left[s, z].astype(jnp.float32))
 
             @pl.when((z > 0) & (z < planes - 1))
             def _():
                 sides = from_left[s, z].astype(jnp.float32) + from_right[s, z].astype(jnp.float32)
-                part_out[s] = (mine + sides).astype(jnp.bfloat16)
+                store(mine + sides)
 
         return carry
+
+    for way in range(2):
+
+        @pl.when(gather_sends(way, 0))
+        def _():
+            gather(way, 0, 0).start()
 
     lax.fori_loop(0, stages + 2 * hops + 1, step, 0)
     for a, result in enumerate((layer_out, grad_out)):
@@ -479,15 +504,16 @@
     bf16, dma = jnp.bfloat16, pltpu.SemaphoreType.DMA
     full = (stages, planes, slice_rows, 3 * width)
     vmem = pl.BlockSpec(memory_space=pltpu.VMEM)
-    parts, layer_output, token_grads = pl.pallas_call(
+    lift_grads, down_grads, layer_output, token_grads = pl.pallas_call(
         functools.partial(fused, owners, planes, per_expert),
         out_shape=(
-            jax.ShapeDtypeStruct(packed.shape, bf16),
+            jax.ShapeDtypeStruct(lift_weights.shape, bf16),
+            jax.ShapeDtypeStruct(down_weights.shape, bf16),
             jax.ShapeDtypeStruct(tokens.shape, bf16),
             jax.ShapeDtypeStruct(tokens.shape, bf16),
         ),
         in_specs=[vmem] * 4,
-        out_specs=[vmem] * 3,
+        out_specs=[vmem] * 4,
         scratch_shapes=[
             pltpu.VMEM(full, bf16),
             pltpu.VMEM(full, bf16),
@@ -505,9 +531,9 @@
             pltpu.VMEM((2, chips, tok_rows, model_width), bf16),
             pltpu.VMEM((2, chips, tok_rows, model_width), bf16),
             dma((3 + stages,)),
-            dma((2, planes)),
             dma((2, planes, stages)),
-            dma((2,)),
+            dma((2, planes, stages)),
+            dma((2, stages)),
             dma((2, stages)),
             dma((3, chips)),
             dma((3, chips)),
@@ -522,10 +548,6 @@
             collective_id=0, has_side_effects=True, vmem_limit_bytes=60 * 1024 * 1024
         ),
     )(tokens, cotangent, gates, packed)
-    parts = parts.reshape(experts, per_expert, slice_rows, 3, width)
-    parts = jnp.transpose(parts, (0, 2, 3, 1, 4)).reshape(experts, slice_rows, 3 * hidden_width)
-    lift_grads = parts[:, :, : 2 * hidden_width]
-    down_grads = jnp.transpose(parts[:, :, 2 * hidden_width :], (0, 2, 1))
     return (layer_output, token_grads, lift_grads, down_grads)
 
 

time: 176 us -> 154 us (0.88)
  Pallas kernels: 164 us -> 142 us
    pallas_call x1, Pallas kernels: 164 us -> 142 us  [dense_shards(): pl.pallas_call(functools.partial(fused, owners, planes, per_expert), out_...]
    unnamed x12 -> x13, local copies, waits for them, and re-layouts: 5.6 us -> 8.12 us
where the time goes in v3:
time: 154 us; the launch traced here: 153 us
  Pallas kernels  142 us (92%)
  local copies, waits for them, and re-layouts  9.63 us (6%)
    pallas_call x1, Pallas kernels, dense_shards(): pl.pallas_call(functools.partial(fused, owners, planes, per_expert), out_...  142 us
    unnamed x13, local copies, waits for them, and re-layouts  8.12 us

profile of v3, /device:TPU:0, one launch (start us, length us, event | category | flops | bytes accessed | tf_op | source)
XLA Modules:
  0.0 153.4 jit_solution(1405295300451606999)
XLA Ops:
  0.6 0.0 copy-start.1
  0.6 0.8 copy.19
  1.5 0.8 copy.20
  2.3 1.0 select_reduce_fusion.refs_2_
  3.2 1.4 copy.21
  4.6 0.0 copy-done.1
  4.7 0.1 pad_maximum_fusion
  4.7 0.1 copy.22
  4.8 1.4 copy.23.refs_3_
  6.3 142.0 %shard_map.93 = (bf16[2,256,768]{2,1,0:T(8,128)(2,1)}, bf16[2,384,256]{2,1,0:T(8,128)(2,1)}, bf16[128,1024]{1,0:T(8,128)(2,1)}, bf16[128,1024]{1,0:T(8,128)(2,1)}) custom-call(bf16[128,1024]{1,0:T(8,128)(2,1)} %refs_0_.1, bf16[128,1024]{1,0:T(8,128)(2,1)} %refs_1_.1, f32[128,128]{1,0:T(8,128)} %select_reduce_fusion.refs_2_, bf16[6,256,384]{2,1,0:T(8,128)(2,1)} %copy.23.refs_3_), custom_call_target="tpu_custom_call" | custom-call | tf_op jit(solution)/shard_map/pallas_call | solution.py:507
  148.3 0.0 copy-start
  148.3 1.7 %copy.28 = bf16[128,1024]{1,0:T(8,128)(2,1)} copy(bf16[128,1024]{1,0:T(8,128)(2,1)} %get-tuple-element.16) | data formatting | bytes 524288
  150.0 0.0 copy-start.2
  150.0 1.7 %copy.29 = bf16[128,1024]{1,0:T(8,128)(2,1)} copy(bf16[128,1024]{1,0:T(8,128)(2,1)} %get-tuple-element.17) | data formatting | bytes 524288
  151.7 0.0 copy-done
  151.7 0.9 copy.30
  152.6 0.0 copy-done.2
  152.6 0.7 copy.31
Async XLA Ops:
  0.6 4.0 %copy-start.1 = (bf16[2,384,256]{2,1,0:T(8,128)(2,1)S(1)}, bf16[2,384,256]{2,1,0:T(8,128)(2,1)}, u32[]{:S(2)}) copy-start(bf16[2,384,256]{2,1,0:T(8,128)(2,1)} %param.10) | copy-start | bytes 1179652
  148.3 3.5 %copy-start = (bf16[2,256,768]{2,1,0:T(8,128)(2,1)S(1)}, bf16[2,256,768]{2,1,0:T(8,128)(2,1)}, u32[]{:S(2)}) copy-start(bf16[2,256,768]{2,1,0:T(8,128)(2,1)} %get-tuple-element.18) | copy-start | bytes 2359300
  150.0 2.6 %copy-start.2 = (bf16[2,384,256]{2,1,0:T(8,128)(2,1)S(1)}, bf16[2,384,256]{2,1,0:T(8,128)(2,1)}, u32[]{:S(2)}) copy-start(bf16[2,384,256]{2,1,0:T(8,128)(2,1)} %get-tuple-element.19) | copy-start | bytes 1179652
